TPU v7x, 32 devices: a whole 2x2x4 slice. The times are simulated.
32 devices in a mesh: ia: 4 (over y, core), ja: 2 (over x), ka: 4 (over z).
Axes of the slice: x: 2, y: 2, z: 4, core: 2. Of those that a mesh axis runs over, the one named last changes fastest.
Arguments:
- block_coords: int32 [4, 2, 4, 4, 3], P('ia', 'ja', 'ka'), may hold values from 0 to 3, as said below
- live_blocks: int32 [4, 2, 4], P('ia', 'ja', 'ka'), may hold values from 1 to 4, as said below
- counts: int32 [4, 2, 4, 4, 64, 4096], P('ia', 'ja', 'ka'), may hold values from 0 to 7
- factor_a: float32 [1024, 256], P(('ia', 'ja', 'ka')), may hold values from 0.3 to 9.6
- factor_b: float32 [512, 256], P(('ja', 'ka')), may hold values from 0.05 to 8
- factor_c: float32 [1024, 256], P('ka', 'ia'), may hold values from 0.05 to 8
Outputs:
- factor_new: float32 [1024, 256], P(('ia', 'ja', 'ka'))
Inputs may be any that keep to these rules, and one draw needn't show every extreme that they name: `block_coords`: a device's slots name distinct blocks; slot 0 is always live, and every mode-1 block of the slab has a live block on some device. `live_blocks`: on some device all 4 slots are live.
All inputs are finite; a program needn't handle non-finite values.
Results may differ from a plain program's by a relative error of at most 0.00061.
Values may be sent and summed in bfloat16 or wider, within the bound.
A program may use at most 64 MiB of HBM per device.

v0:
```python
import jax
import jax.numpy as jnp
from jax import lax
from jax.sharding import PartitionSpec as P

R = 256
BS = 64
RB1 = 4
RB2 = 4
RB3 = 4
SLOTS = 4


def make_panel(rows_b, rows_c, index_j, index_k):
    piece_b = lax.dynamic_slice_in_dim(rows_b, index_j * BS, BS, 0)
    piece_c = lax.dynamic_slice_in_dim(rows_c, index_k * BS, BS, 0)
    return (piece_b[:, None, :] * piece_c[None, :, :]).reshape(BS * BS, R).astype(jnp.bfloat16)


def add_block(phi, factor_low, panel, index_i, weight, block_counts):
    block_a = lax.dynamic_slice_in_dim(factor_low, index_i * BS, BS, 0)
    model = lax.dot_general(
        block_a, panel, (((1,), (1,)), ((), ())), preferred_element_type=jnp.float32
    )
    ratio = (block_counts.astype(jnp.float32) / model).astype(jnp.bfloat16)
    part = jnp.dot(ratio, panel, preferred_element_type=jnp.float32) * weight
    old = lax.dynamic_slice_in_dim(phi, index_i * BS, BS, 0)
    return lax.dynamic_update_slice_in_dim(phi, old + part, index_i * BS, 0)


def local(block_coords, live_blocks, counts, factor_a, factor_b, factor_c):
    coords = block_coords.reshape(SLOTS, 3)
    local_counts = counts.reshape(SLOTS, BS, BS * BS)
    weights = (jnp.arange(SLOTS, dtype=jnp.int32) < live_blocks.reshape(())).astype(jnp.float32)
    rows_b = lax.all_gather(factor_b, "ka", axis=0, tiled=True)
    rows_c = lax.all_gather(factor_c, "ia", axis=1, tiled=True)
    sums_b = rows_b.reshape(RB2, BS, R).sum(axis=1)
    sums_c = rows_c.reshape(RB3, BS, R).sum(axis=1)
    pick_j = (coords[:, 1:2] == jnp.arange(RB2, dtype=jnp.int32)[None, :]).astype(jnp.float32)
    pick_k = (coords[:, 2:3] == jnp.arange(RB3, dtype=jnp.int32)[None, :]).astype(jnp.float32)
    masses = jnp.dot(pick_j, sums_b, precision=lax.Precision.HIGHEST) * jnp.dot(
        pick_k, sums_c, precision=lax.Precision.HIGHEST
    )
    pick_i = (coords[:, 0:1] == jnp.arange(RB1, dtype=jnp.int32)[None, :]).astype(
        jnp.float32
    ) * weights[:, None]
    mass_part = lax.dot_general(
        pick_i, masses, (((0,), (0,)), ((), ())), precision=lax.Precision.HIGHEST
    )
    mass = lax.psum(mass_part, ("ja", "ka"))
    mass_rows = jnp.broadcast_to(mass[:, None, :], (RB1, BS, R)).reshape(RB1 * BS, R)
    owned = factor_a.shape[0]
    first_row = lax.axis_index(("ja", "ka")) * owned
    my_mass = lax.dynamic_slice_in_dim(mass_rows, first_row, owned, 0)
    empty = jnp.zeros((RB1 * BS, R), jnp.float32)

    def accumulate(factor_low):

        def step(phi, item):
            index_i, index_j, index_k, weight, block_counts = item
            panel = make_panel(rows_b, rows_c, index_j, index_k)
            return (add_block(phi, factor_low, panel, index_i, weight, block_counts), None)

        phi, _ = lax.scan(
            step, empty, (coords[:, 0], coords[:, 1], coords[:, 2], weights, local_counts)
        )
        return phi

    whole = lax.all_gather(factor_a, ("ja", "ka"), axis=0, tiled=True)
    phi = accumulate(whole.astype(jnp.bfloat16))
    totals = lax.psum(phi, ("ja", "ka"))
    updated = whole * totals / mass_rows
    phi = accumulate(updated.astype(jnp.bfloat16))
    mine = lax.psum_scatter(phi, ("ja", "ka"), scatter_dimension=0, tiled=True)
    return lax.dynamic_slice_in_dim(updated, first_row, owned, 0) * mine / my_mass


def solution(mesh):
    placed = (
        P("ia", "ja", "ka", None, None),
        P("ia", "ja", "ka"),
        P("ia", "ja", "ka", None, None, None),
        P(("ia", "ja", "ka"), None),
        P(("ja", "ka"), None),
        P("ka", "ia"),
    )
    return jax.shard_map(
        local, mesh=mesh, in_specs=placed, out_specs=P(("ia", "ja", "ka"), None), check_vma=False
    )
```

profile of v0, /device:TPU:0, one launch (start us, length us, event | category | flops | bytes accessed | tf_op | source)
XLA Modules:
  0.0 275.6 jit_solution(7233616077265290646)
XLA Ops:
  6.5 0.8 copy.14
  7.3 0.2 slice_reduce_fusion.2
  7.5 7.5 %all_gather.11 = f32[256,256]{0,1:T(8,128)S(1)} all-gather(f32[256,64]{0,1:T(8,128)} %param.15), channel_id=1, replica_groups=mesh['ia'=4,'ja'=2,'ka'=4] {'ia'}, dimensions={1}, use_global_device_ids=true | all-gather | bytes 327680 | tf_op jit(solution)/shard_map/all_gather | solution.py:36
  15.1 14.3 %all_gather.10 = f32[256,256]{1,0:T(8,128)S(1)} all-gather(f32[64,256]{1,0:T(8,128)} %param.14), channel_id=1, replica_groups=mesh['ia'=4,'ja'=2,'ka'=4] {'ka'}, dimensions={0}, use_global_device_ids=true | all-gather | bytes 327680 | tf_op jit(solution)/shard_map/all_gather | solution.py:35
  30.1 31.8 %all_gather.9 = f32[256,256]{1,0:T(8,128)S(1)} all-gather(f32[32,256]{1,0:T(8,128)} %param.13), channel_id=1, replica_groups=mesh['ia'=4,'ja'=2,'ka'=4] {'ja','ka'}, dimensions={0}, use_global_device_ids=true | all-gather | bytes 294912 | tf_op jit(solution)/shard_map/all_gather | solution.py:69
  62.0 34.4 %while.20 = (s32[]{:T(128)}, f32[256,256]{1,0:T(8,128)S(1)}, s32[4]{0:T(128)S(1)}, s32[4,64,4096]{2,1,0:T(8,128)}, bf16[256,256]{1,0:T(8,128)(2,1)S(1)}, /*index...) while((s32[]{:T(128)}, f32[256,256]{1,0:T(8,128)S(1)}, ...), condition=%wide.region_1.0_spmd, body=%wide.region_0.0_spmd.sunk | while | flops 271351808 | bytes 7899463 | solution.py:64
  62.0 0.7 dynamic_slice.108
  63.3 0.7 dynamic_slice.109
  64.7 0.7 multiply_convert_fusion.4
  65.4 0.7 dynamic_slice.107
  66.8 0.7 dynamic_slice.110
  67.5 3.1 %fusion.52 = f32[256,256]{1,0:T(8,128)S(1)} fusion(f32[256,256]{1,0:T(8,128)S(1)} %get-tuple-element.345, s32[]{:T(128)S(6)} %select_n.33, bf16[4096,256]{1,0:T(8,128)(2,1)S(1)} %bitcast.70, s32[4,64,4096]{2,1,0:T(8,128)} %get-tuple-element.361, s32[]{:T(128)} %get-tuple-element.344, f32[]{:T(128)} %bitcast.60, ...), kind=kOutput, calls=%fused_computation.6.clone.1 | convolution fusion | flops 269254656 | bytes 5408768 | tf_op jit(solution)/shard_map/while/body/eval_jaxpr/dot_general | solution.py:26
  70.6 0.7 dynamic_slice.108
  71.9 0.7 dynamic_slice.109
  73.3 0.7 multiply_convert_fusion.4
  74.0 0.7 dynamic_slice.107
  75.4 0.7 dynamic_slice.110
  76.1 3.1 %fusion.52 = f32[256,256]{1,0:T(8,128)S(1)} fusion(f32[256,256]{1,0:T(8,128)S(1)} %get-tuple-element.345, s32[]{:T(128)S(6)} %select_n.33, bf16[4096,256]{1,0:T(8,128)(2,1)S(1)} %bitcast.70, s32[4,64,4096]{2,1,0:T(8,128)} %get-tuple-element.361, s32[]{:T(128)} %get-tuple-element.344, f32[]{:T(128)} %bitcast.60, ...), kind=kOutput, calls=%fused_computation.6.clone.1 | convolution fusion | flops 269254656 | bytes 5408768 | tf_op jit(solution)/shard_map/while/body/eval_jaxpr/dot_general | solution.py:26
  79.2 0.7 dynamic_slice.108
  80.5 0.7 dynamic_slice.109
  81.9 0.7 multiply_convert_fusion.4
  82.6 0.7 dynamic_slice.107
  84.0 0.7 dynamic_slice.110
  84.7 3.1 %fusion.52 = f32[256,256]{1,0:T(8,128)S(1)} fusion(f32[256,256]{1,0:T(8,128)S(1)} %get-tuple-element.345, s32[]{:T(128)S(6)} %select_n.33, bf16[4096,256]{1,0:T(8,128)(2,1)S(1)} %bitcast.70, s32[4,64,4096]{2,1,0:T(8,128)} %get-tuple-element.361, s32[]{:T(128)} %get-tuple-element.344, f32[]{:T(128)} %bitcast.60, ...), kind=kOutput, calls=%fused_computation.6.clone.1 | convolution fusion | flops 269254656 | bytes 5408768 | tf_op jit(solution)/shard_map/while/body/eval_jaxpr/dot_general | solution.py:26
  87.8 0.7 dynamic_slice.108
  89.2 0.7 dynamic_slice.109
  90.5 0.7 multiply_convert_fusion.4
  91.2 0.7 dynamic_slice.107
  92.6 0.7 dynamic_slice.110
  93.3 3.1 %fusion.52 = f32[256,256]{1,0:T(8,128)S(1)} fusion(f32[256,256]{1,0:T(8,128)S(1)} %get-tuple-element.345, s32[]{:T(128)S(6)} %select_n.33, bf16[4096,256]{1,0:T(8,128)(2,1)S(1)} %bitcast.70, s32[4,64,4096]{2,1,0:T(8,128)} %get-tuple-element.361, s32[]{:T(128)} %get-tuple-element.344, f32[]{:T(128)} %bitcast.60, ...), kind=kOutput, calls=%fused_computation.6.clone.1 | convolution fusion | flops 269254656 | bytes 5408768 | tf_op jit(solution)/shard_map/while/body/eval_jaxpr/dot_general | solution.py:26
  96.4 0.7 copy-done.1
  97.4 0.2 convolution_multiply_fusion
  97.6 0.3 fusion.24
  97.9 21.7 %psum.15 = f32[4,256]{1,0:T(4,128)S(1)} all-reduce(f32[4,256]{1,0:T(4,128)S(1)} %fusion.24), channel_id=1, replica_groups=mesh['ia'=4,'ja'=2,'ka'=4] {'ja','ka'}, use_global_device_ids=true, to_apply=%region_5.6 | all-reduce | flops 1024 | bytes 8192 | tf_op jit(solution)/shard_map/psum | solution.py:50
  119.5 49.9 %all-reduce.2.cloned.1.call-done = f32[256,256]{1,0:T(8,128)} async-done(((f32[256,256]{1,0:T(8,128)}), f32[256,256]{1,0:T(8,128)}) %all-reduce.2.cloned.1.call-update) | async-done | bytes 262160 | tf_op jit(solution)/shard_map/psum | solution.py:71
  169.4 1.0 fusion.33
  170.5 34.4 %while.21 = (s32[]{:T(128)}, f32[256,256]{1,0:T(8,128)S(1)}, s32[4]{0:T(128)S(1)}, s32[4,64,4096]{2,1,0:T(8,128)}, bf16[256,256]{1,0:T(8,128)(2,1)S(1)}, /*index...) while((s32[]{:T(128)}, f32[256,256]{1,0:T(8,128)S(1)}, ...), condition=%wide.region_7.8_spmd, body=%wide.region_6.7_spmd.sunk | while | flops 271351808 | bytes 7899463 | solution.py:64
  170.5 0.7 dynamic_slice.116
  171.8 0.7 dynamic_slice.117
  173.2 0.7 multiply_convert_fusion.5
  173.9 0.7 dynamic_slice.115
  175.3 0.7 dynamic_slice.118
  176.0 3.1 %fusion.56 = f32[256,256]{1,0:T(8,128)S(1)} fusion(f32[256,256]{1,0:T(8,128)S(1)} %get-tuple-element.387, s32[]{:T(128)S(6)} %select_n.36, bf16[4096,256]{1,0:T(8,128)(2,1)S(1)} %bitcast.71, s32[4,64,4096]{2,1,0:T(8,128)} %get-tuple-element.403, s32[]{:T(128)} %get-tuple-element.386, f32[]{:T(128)} %bitcast.68, ...), kind=kOutput, calls=%fused_computation.20.clone.1 | convolution fusion | flops 269254656 | bytes 5408768 | tf_op jit(solution)/shard_map/while/body/eval_jaxpr/dot_general | solution.py:26
  179.1 0.7 dynamic_slice.116
  180.4 0.7 dynamic_slice.117
  181.8 0.7 multiply_convert_fusion.5
  182.5 0.7 dynamic_slice.115
  183.9 0.7 dynamic_slice.118
  184.6 3.1 %fusion.56 = f32[256,256]{1,0:T(8,128)S(1)} fusion(f32[256,256]{1,0:T(8,128)S(1)} %get-tuple-element.387, s32[]{:T(128)S(6)} %select_n.36, bf16[4096,256]{1,0:T(8,128)(2,1)S(1)} %bitcast.71, s32[4,64,4096]{2,1,0:T(8,128)} %get-tuple-element.403, s32[]{:T(128)} %get-tuple-element.386, f32[]{:T(128)} %bitcast.68, ...), kind=kOutput, calls=%fused_computation.20.clone.1 | convolution fusion | flops 269254656 | bytes 5408768 | tf_op jit(solution)/shard_map/while/body/eval_jaxpr/dot_general | solution.py:26
  187.7 0.7 dynamic_slice.116
  189.0 0.7 dynamic_slice.117
  190.4 0.7 multiply_convert_fusion.5
  191.1 0.7 dynamic_slice.115
  192.5 0.7 dynamic_slice.118
  193.2 3.1 %fusion.56 = f32[256,256]{1,0:T(8,128)S(1)} fusion(f32[256,256]{1,0:T(8,128)S(1)} %get-tuple-element.387, s32[]{:T(128)S(6)} %select_n.36, bf16[4096,256]{1,0:T(8,128)(2,1)S(1)} %bitcast.71, s32[4,64,4096]{2,1,0:T(8,128)} %get-tuple-element.403, s32[]{:T(128)} %get-tuple-element.386, f32[]{:T(128)} %bitcast.68, ...), kind=kOutput, calls=%fused_computation.20.clone.1 | convolution fusion | flops 269254656 | bytes 5408768 | tf_op jit(solution)/shard_map/while/body/eval_jaxpr/dot_general | solution.py:26
  196.3 0.7 dynamic_slice.116
  197.6 0.7 dynamic_slice.117
  199.0 0.7 multiply_convert_fusion.5
  199.7 0.7 dynamic_slice.115
  201.1 0.7 dynamic_slice.118
  201.8 3.1 %fusion.56 = f32[256,256]{1,0:T(8,128)S(1)} fusion(f32[256,256]{1,0:T(8,128)S(1)} %get-tuple-element.387, s32[]{:T(128)S(6)} %select_n.36, bf16[4096,256]{1,0:T(8,128)(2,1)S(1)} %bitcast.71, s32[4,64,4096]{2,1,0:T(8,128)} %get-tuple-element.403, s32[]{:T(128)} %get-tuple-element.386, f32[]{:T(128)} %bitcast.68, ...), kind=kOutput, calls=%fused_computation.20.clone.1 | convolution fusion | flops 269254656 | bytes 5408768 | tf_op jit(solution)/shard_map/while/body/eval_jaxpr/dot_general | solution.py:26
  204.9 0.7 copy-done
  205.6 61.8 %reduce-scatter.2.cloned.1.call-done = f32[32,256]{1,0:T(8,128)} async-done(((f32[256,256]{1,0:T(8,128)}), f32[32,256]{1,0:T(8,128)}) %reduce-scatter.2.cloned.1.call-update) | async-done | bytes 32784 | tf_op jit(solution)/shard_map/reduce_scatter | solution.py:74
  267.4 1.4 dynamic-slice_divide_fusion
  (23 shorter events, 0.7 us)
Async XLA Ops:
  6.5 162.9 %all-reduce.2.cloned.1.call-start = ((), (), s32[]{:S(2)}) async-start(), calls=%async_computation.1 | async-start | bytes 524288 | tf_op jit(solution)/shard_map/psum | solution.py:71
  96.4 0.7 copy-start.1
  97.1 170.3 %reduce-scatter.2.cloned.1.call-start = ((), (), s32[]{:S(2)}) async-start(), calls=%async_computation.2 | async-start | bytes 294912 | tf_op jit(solution)/shard_map/reduce_scatter | solution.py:74
  204.9 0.7 copy-start
Sparse Core Ops, SparseCore 0:
  97.2 72.1 all-reduce.1
  205.7 61.6 reduce-scatter.1
where the time goes:
time: 277 us; the launch traced here: 276 us
  waiting for transfers between devices  112 us (40%)
  blocking collectives  75.3 us (27%)
  matrix products  25.4 us (9%)
  local copies, waits for them, and re-layouts  24 us (9%)
  loops' own time  17.1 us (6%)
  between operations  14.1 us (5%)
  other arithmetic  7.95 us (3%)
    reduce_scatter x1, waiting for transfers between devices, local(): mine = lax.psum_scatter(phi, ('ja', 'ka'), scatter_dimension=0, tiled=True)  61.8 us
    psum x1, waiting for transfers between devices, local(): totals = lax.psum(phi, ('ja', 'ka'))  49.9 us
    all_gather x1, blocking collectives, local(): whole = lax.all_gather(factor_a, ('ja', 'ka'), axis=0, tiled=True)  31.8 us
    dot_general x8, matrix products, add_block(): part = jnp.dot(ratio, panel, preferred_element_type=jnp.float32) * weight  24.7 us
    psum x1, blocking collectives, local(): mass = lax.psum(mass_part, ('ja', 'ka'))  21.7 us
    dynamic_slice x32, local copies, waits for them, and re-layouts, accumulate(): lax.scan(step, empty, (coords[:, 0], coords[:, 1], coords[:, 2], weights,...  21.4 us
    another operation x2, loops' own time, accumulate(): lax.scan(step, empty, (coords[:, 0], coords[:, 1], coords[:, 2], weights,...  17.1 us
    all_gather x1, blocking collectives, local(): rows_b = lax.all_gather(factor_b, 'ka', axis=0, tiled=True)  14.3 us
  transfers between devices with their start and end apart: 2, of which 2 were waited for; matrix products, arithmetic and copies ran while one was open for 0% of the time, Pallas kernels for 0%

commit v1 on v0

--- a/solution.py
+++ b/solution.py
@@ -68,7 +68,8 @@
 
     whole = lax.all_gather(factor_a, ("ja", "ka"), axis=0, tiled=True)
     phi = accumulate(whole.astype(jnp.bfloat16))
-    totals = lax.psum(phi, ("ja", "ka"))
+    parts = lax.all_gather(phi, ("ja", "ka"), axis=0, tiled=False)
+    totals = parts.sum(axis=0)
     updated = whole * totals / mass_rows
     phi = accumulate(updated.astype(jnp.bfloat16))
     mine = lax.psum_scatter(phi, ("ja", "ka"), scatter_dimension=0, tiled=True)

time: 277 us -> 255 us (0.921)
  waiting for transfers between devices: 112 us -> 89 us
    psum x1 -> x0, waiting for transfers between devices: 49.9 us -> none  [local(): totals = lax.psum(phi, ('ja', 'ka'))]
    all_gather x0 -> x1, waiting for transfers between devices: none -> 27.8 us  [local(): parts = lax.all_gather(phi, ('ja', 'ka'), axis=0, tiled=False)]
where the time goes in v1:
time: 255 us; the launch traced here: 254 us
  waiting for transfers between devices  89 us (35%)
  blocking collectives  75.4 us (30%)
  matrix products  25.4 us (10%)
  local copies, waits for them, and re-layouts  24.1 us (9%)
  loops' own time  17.1 us (7%)
  between operations  14.1 us (6%)
  other arithmetic  8.74 us (3%)
    reduce_scatter x1, waiting for transfers between devices, local(): mine = lax.psum_scatter(phi, ('ja', 'ka'), scatter_dimension=0, tiled=True)  61.1 us
    all_gather x1, blocking collectives, local(): whole = lax.all_gather(factor_a, ('ja', 'ka'), axis=0, tiled=True)  31.8 us
    all_gather x1, waiting for transfers between devices, local(): parts = lax.all_gather(phi, ('ja', 'ka'), axis=0, tiled=False)  27.8 us
    dot_general x8, matrix products, add_block(): part = jnp.dot(ratio, panel, preferred_element_type=jnp.float32) * weight  24.7 us
    psum x1, blocking collectives, local(): mass = lax.psum(mass_part, ('ja', 'ka'))  21.8 us
    dynamic_slice x32, local copies, waits for them, and re-layouts, accumulate(): lax.scan(step, empty, (coords[:, 0], coords[:, 1], coords[:, 2], weights,...  21.4 us
    another operation x2, loops' own time, accumulate(): lax.scan(step, empty, (coords[:, 0], coords[:, 1], coords[:, 2], weights,...  17.1 us
    all_gather x1, blocking collectives, local(): rows_b = lax.all_gather(factor_b, 'ka', axis=0, tiled=True)  14.3 us
  transfers between devices with their start and end apart: 2, of which 2 were waited for; matrix products, arithmetic and copies ran while one was open for 0% of the time, Pallas kernels for 0%

profile of v1, /device:TPU:0, one launch (start us, length us, event | category | flops | bytes accessed | tf_op | source)
XLA Modules:
  0.0 253.9 jit_solution(866820324215561421)
XLA Ops:
  6.5 0.8 copy.14
  7.3 0.2 slice_reduce_fusion.2
  7.5 7.5 %all_gather.17 = f32[256,256]{0,1:T(8,128)S(1)} all-gather(f32[256,64]{0,1:T(8,128)} %param.15), channel_id=1, replica_groups=mesh['ia'=4,'ja'=2,'ka'=4] {'ia'}, dimensions={1}, use_global_device_ids=true | all-gather | bytes 327680 | tf_op jit(solution)/shard_map/all_gather | solution.py:36
  15.1 14.3 %all_gather.16 = f32[256,256]{1,0:T(8,128)S(1)} all-gather(f32[64,256]{1,0:T(8,128)} %param.14), channel_id=1, replica_groups=mesh['ia'=4,'ja'=2,'ka'=4] {'ka'}, dimensions={0}, use_global_device_ids=true | all-gather | bytes 327680 | tf_op jit(solution)/shard_map/all_gather | solution.py:35
  30.1 31.8 %all_gather.15 = f32[256,256]{1,0:T(8,128)S(1)} all-gather(f32[32,256]{1,0:T(8,128)} %param.13), channel_id=1, replica_groups=mesh['ia'=4,'ja'=2,'ka'=4] {'ja','ka'}, dimensions={0}, use_global_device_ids=true | all-gather | bytes 294912 | tf_op jit(solution)/shard_map/all_gather | solution.py:69
  62.0 34.4 %while.20 = (s32[]{:T(128)}, f32[256,256]{1,0:T(8,128)S(1)}, s32[4]{0:T(128)S(1)}, s32[4,64,4096]{2,1,0:T(8,128)}, bf16[256,256]{1,0:T(8,128)(2,1)S(1)}, /*index...) while((s32[]{:T(128)}, f32[256,256]{1,0:T(8,128)S(1)}, ...), condition=%wide.region_1.0_spmd, body=%wide.region_0.0_spmd.sunk | while | flops 271351808 | bytes 7899463 | solution.py:64
  62.0 0.7 dynamic_slice.108
  63.3 0.7 dynamic_slice.109
  64.7 0.7 multiply_convert_fusion.4
  65.4 0.7 dynamic_slice.107
  66.8 0.7 dynamic_slice.110
  67.5 3.1 %fusion.52 = f32[256,256]{1,0:T(8,128)S(1)} fusion(f32[256,256]{1,0:T(8,128)S(1)} %get-tuple-element.345, s32[]{:T(128)S(6)} %select_n.33, bf16[4096,256]{1,0:T(8,128)(2,1)S(1)} %bitcast.71, s32[4,64,4096]{2,1,0:T(8,128)} %get-tuple-element.361, s32[]{:T(128)} %get-tuple-element.344, f32[]{:T(128)} %bitcast.61, ...), kind=kOutput, calls=%fused_computation.6.clone.1 | convolution fusion | flops 269254656 | bytes 5408768 | tf_op jit(solution)/shard_map/while/body/eval_jaxpr/dot_general | solution.py:26
  70.6 0.7 dynamic_slice.108
  71.9 0.7 dynamic_slice.109
  73.3 0.7 multiply_convert_fusion.4
  74.0 0.7 dynamic_slice.107
  75.4 0.7 dynamic_slice.110
  76.1 3.1 %fusion.52 = f32[256,256]{1,0:T(8,128)S(1)} fusion(f32[256,256]{1,0:T(8,128)S(1)} %get-tuple-element.345, s32[]{:T(128)S(6)} %select_n.33, bf16[4096,256]{1,0:T(8,128)(2,1)S(1)} %bitcast.71, s32[4,64,4096]{2,1,0:T(8,128)} %get-tuple-element.361, s32[]{:T(128)} %get-tuple-element.344, f32[]{:T(128)} %bitcast.61, ...), kind=kOutput, calls=%fused_computation.6.clone.1 | convolution fusion | flops 269254656 | bytes 5408768 | tf_op jit(solution)/shard_map/while/body/eval_jaxpr/dot_general | solution.py:26
  79.2 0.7 dynamic_slice.108
  80.5 0.7 dynamic_slice.109
  81.9 0.7 multiply_convert_fusion.4
  82.6 0.7 dynamic_slice.107
  84.0 0.7 dynamic_slice.110
  84.7 3.1 %fusion.52 = f32[256,256]{1,0:T(8,128)S(1)} fusion(f32[256,256]{1,0:T(8,128)S(1)} %get-tuple-element.345, s32[]{:T(128)S(6)} %select_n.33, bf16[4096,256]{1,0:T(8,128)(2,1)S(1)} %bitcast.71, s32[4,64,4096]{2,1,0:T(8,128)} %get-tuple-element.361, s32[]{:T(128)} %get-tuple-element.344, f32[]{:T(128)} %bitcast.61, ...), kind=kOutput, calls=%fused_computation.6.clone.1 | convolution fusion | flops 269254656 | bytes 5408768 | tf_op jit(solution)/shard_map/while/body/eval_jaxpr/dot_general | solution.py:26
  87.8 0.7 dynamic_slice.108
  89.2 0.7 dynamic_slice.109
  90.5 0.7 multiply_convert_fusion.4
  91.2 0.7 dynamic_slice.107
  92.6 0.7 dynamic_slice.110
  93.3 3.1 %fusion.52 = f32[256,256]{1,0:T(8,128)S(1)} fusion(f32[256,256]{1,0:T(8,128)S(1)} %get-tuple-element.345, s32[]{:T(128)S(6)} %select_n.33, bf16[4096,256]{1,0:T(8,128)(2,1)S(1)} %bitcast.71, s32[4,64,4096]{2,1,0:T(8,128)} %get-tuple-element.361, s32[]{:T(128)} %get-tuple-element.344, f32[]{:T(128)} %bitcast.61, ...), kind=kOutput, calls=%fused_computation.6.clone.1 | convolution fusion | flops 269254656 | bytes 5408768 | tf_op jit(solution)/shard_map/while/body/eval_jaxpr/dot_general | solution.py:26
  96.4 0.7 copy-done.1
  97.4 0.2 convolution_multiply_fusion
  97.6 0.3 fusion.24
  97.9 21.8 %psum.7 = f32[4,256]{1,0:T(4,128)S(1)} all-reduce(f32[4,256]{1,0:T(4,128)S(1)} %fusion.24), channel_id=1, replica_groups=mesh['ia'=4,'ja'=2,'ka'=4] {'ja','ka'}, use_global_device_ids=true, to_apply=%region_5.6 | all-reduce | flops 1024 | bytes 8192 | tf_op jit(solution)/shard_map/psum | solution.py:50
  119.7 27.8 %all-gather.3.cloned.1.call-done = f32[2048,256]{1,0:T(8,128)} async-done(((f32[256,256]{1,0:T(8,128)}), f32[2048,256]{1,0:T(8,128)}) %all-gather.3.cloned.1.call-update) | async-done | bytes 2097168 | tf_op jit(solution)/shard_map/all_gather | solution.py:71
  147.5 1.8 reduce_sum.27
  149.3 34.4 %while.21 = (s32[]{:T(128)}, f32[256,256]{1,0:T(8,128)S(1)}, s32[4]{0:T(128)S(1)}, s32[4,64,4096]{2,1,0:T(8,128)}, bf16[256,256]{1,0:T(8,128)(2,1)S(1)}, /*index...) while((s32[]{:T(128)}, f32[256,256]{1,0:T(8,128)S(1)}, ...), condition=%wide.region_7.8_spmd, body=%wide.region_6.7_spmd.sunk | while | flops 271351808 | bytes 7899463 | solution.py:64
  149.4 0.7 dynamic_slice.116
  150.7 0.7 dynamic_slice.117
  152.1 0.7 multiply_convert_fusion.5
  152.8 0.7 dynamic_slice.115
  154.2 0.7 dynamic_slice.118
  154.8 3.1 %fusion.56 = f32[256,256]{1,0:T(8,128)S(1)} fusion(f32[256,256]{1,0:T(8,128)S(1)} %get-tuple-element.387, s32[]{:T(128)S(6)} %select_n.36, bf16[4096,256]{1,0:T(8,128)(2,1)S(1)} %bitcast.72, s32[4,64,4096]{2,1,0:T(8,128)} %get-tuple-element.403, s32[]{:T(128)} %get-tuple-element.386, f32[]{:T(128)} %bitcast.69, ...), kind=kOutput, calls=%fused_computation.20.clone.1 | convolution fusion | flops 269254656 | bytes 5408768 | tf_op jit(solution)/shard_map/while/body/eval_jaxpr/dot_general | solution.py:26
  158.0 0.7 dynamic_slice.116
  159.3 0.7 dynamic_slice.117
  160.7 0.7 multiply_convert_fusion.5
  161.4 0.7 dynamic_slice.115
  162.8 0.7 dynamic_slice.118
  163.5 3.1 %fusion.56 = f32[256,256]{1,0:T(8,128)S(1)} fusion(f32[256,256]{1,0:T(8,128)S(1)} %get-tuple-element.387, s32[]{:T(128)S(6)} %select_n.36, bf16[4096,256]{1,0:T(8,128)(2,1)S(1)} %bitcast.72, s32[4,64,4096]{2,1,0:T(8,128)} %get-tuple-element.403, s32[]{:T(128)} %get-tuple-element.386, f32[]{:T(128)} %bitcast.69, ...), kind=kOutput, calls=%fused_computation.20.clone.1 | convolution fusion | flops 269254656 | bytes 5408768 | tf_op jit(solution)/shard_map/while/body/eval_jaxpr/dot_general | solution.py:26
  166.6 0.7 dynamic_slice.116
  167.9 0.7 dynamic_slice.117
  169.3 0.7 multiply_convert_fusion.5
  170.0 0.7 dynamic_slice.115
  171.4 0.7 dynamic_slice.118
  172.1 3.1 %fusion.56 = f32[256,256]{1,0:T(8,128)S(1)} fusion(f32[256,256]{1,0:T(8,128)S(1)} %get-tuple-element.387, s32[]{:T(128)S(6)} %select_n.36, bf16[4096,256]{1,0:T(8,128)(2,1)S(1)} %bitcast.72, s32[4,64,4096]{2,1,0:T(8,128)} %get-tuple-element.403, s32[]{:T(128)} %get-tuple-element.386, f32[]{:T(128)} %bitcast.69, ...), kind=kOutput, calls=%fused_computation.20.clone.1 | convolution fusion | flops 269254656 | bytes 5408768 | tf_op jit(solution)/shard_map/while/body/eval_jaxpr/dot_general | solution.py:26
  175.2 0.7 dynamic_slice.116
  176.5 0.7 dynamic_slice.117
  177.9 0.7 multiply_convert_fusion.5
  178.6 0.7 dynamic_slice.115
  180.0 0.7 dynamic_slice.118
  180.7 3.1 %fusion.56 = f32[256,256]{1,0:T(8,128)S(1)} fusion(f32[256,256]{1,0:T(8,128)S(1)} %get-tuple-element.387, s32[]{:T(128)S(6)} %select_n.36, bf16[4096,256]{1,0:T(8,128)(2,1)S(1)} %bitcast.72, s32[4,64,4096]{2,1,0:T(8,128)} %get-tuple-element.403, s32[]{:T(128)} %get-tuple-element.386, f32[]{:T(128)} %bitcast.69, ...), kind=kOutput, calls=%fused_computation.20.clone.1 | convolution fusion | flops 269254656 | bytes 5408768 | tf_op jit(solution)/shard_map/while/body/eval_jaxpr/dot_general | solution.py:26
  183.8 0.7 copy-done
  184.5 61.1 %reduce-scatter.2.cloned.1.call-done = f32[32,256]{1,0:T(8,128)} async-done(((f32[256,256]{1,0:T(8,128)}), f32[32,256]{1,0:T(8,128)}) %reduce-scatter.2.cloned.1.call-update) | async-done | bytes 32784 | tf_op jit(solution)/shard_map/reduce_scatter | solution.py:75
  245.6 1.4 dynamic-slice_divide_fusion
  (24 shorter events, 0.7 us)
Async XLA Ops:
  6.5 141.0 %all-gather.3.cloned.1.call-start = ((), (), s32[]{:S(2)}) async-start(), calls=%async_computation.2 | async-start | bytes 2359296 | tf_op jit(solution)/shard_map/all_gather | solution.py:71
  96.4 0.7 copy-start.1
  97.1 148.5 %reduce-scatter.2.cloned.1.call-start = ((), (), s32[]{:S(2)}) async-start(), calls=%async_computation.1 | async-start | bytes 294912 | tf_op jit(solution)/shard_map/reduce_scatter | solution.py:75
  183.8 0.7 copy-start
Sparse Core Ops, SparseCore 0:
  97.3 50.2 all-gather.2
  184.6 60.9 reduce-scatter.1
